TPU v7x, 256 devices: a whole 4x4x8 slice. The times are simulated.
256 devices in a mesh: req: 32 (over z, y), head: 8 (over x, core).
Axes of the slice: x: 4, y: 4, z: 8, core: 2. Of those that a mesh axis runs over, the one named last changes fastest.
Arguments:
- hidden: bfloat16 [512, 2048], P('req'), may hold values from -6 to 6
- deal_order: int32 [512], replicated, may hold values from 0 to 511, each once
- lengths: int32 [512], replicated, may hold values from 1 to 8192, as said below
- page_table: int32 [512, 64], replicated, may hold values from 0 to 2047, as said below
- key_cache: bfloat16 [2048, 128, 8, 128], P('req', None, 'head'), as said below
- value_cache: bfloat16 [2048, 128, 8, 128], P('req', None, 'head'), may hold values from -12 to 12
- attn_gain: float32 [2048], replicated, may hold values from 0.1 to 1.9
- w_query: bfloat16 [2048, 2048], P(None, 'head'), may hold values from -0.125 to 0.125
- w_key: bfloat16 [2048, 1024], P(None, 'head'), may hold values from -0.125 to 0.125
- w_value: bfloat16 [2048, 1024], P(None, 'head'), may hold values from -0.125 to 0.125
- w_gate: bfloat16 [2048, 2048], P(None, 'head'), may hold values from -0.125 to 0.125
- w_out: bfloat16 [2048, 2048], P('head'), may hold values from -1.5 to 1.5
- query_gain: float32 [128], replicated, may hold values from 0.5 to 2
- key_gain: float32 [128], replicated, may hold values from 0.5 to 2
- mlp_gain: float32 [2048], replicated, may hold values from 0.1 to 1.9
- mlp_gate: bfloat16 [2048, 3072], P(None, 'head'), may hold values from -0.125 to 0.125
- mlp_up: bfloat16 [2048, 3072], P(None, 'head'), may hold values from -0.125 to 0.125
- mlp_down: bfloat16 [3072, 2048], P('head'), may hold values from -0.109375 to 0.109375
Outputs:
- output: bfloat16 [512, 2048], P('req')
Inputs may be any that keep to these rules, and one draw needn't show every extreme that they name: `lengths`: one request holds exactly 8192 cached tokens, and all requests together fill at most 2048 pages of 128 tokens. `page_table`: for request r the first ceil(lengths[r] / 128) entries of row r name, in order, the pages that hold its cached tokens; no page is named by two such entries; the other entries are arbitrary page numbers. `key_cache`: cached keys; entries lie within -402 and 402.
All inputs are finite; a program needn't handle non-finite values.
Results may differ from a plain program's by a relative error of at most 0.022.
Values may be sent and summed in bfloat16 or wider, within the bound.
A program may use at most 64 MiB of HBM per device.

v0:
```python
import math
import jax
import jax.numpy as jnp
from jax import lax
from jax.sharding import PartitionSpec as P

EPSILON = 1e-06
ROPE_BASE = 1000000.0
LOW_SCORE = -1e30
LOG_TWO = math.log(2.0)


def rms_inv(values):
    return lax.rsqrt(jnp.mean(values * values, axis=-1, keepdims=True) + EPSILON)


def rotate(values, position):
    half_dim = values.shape[-1] // 2
    exponent = jnp.arange(half_dim, dtype=jnp.float32) * (2.0 / values.shape[-1])
    frequency = ROPE_BASE ** (-exponent)
    angles = position[:, None] * frequency[None, :]
    ones_tail = (1,) * (values.ndim - 2)
    angles = angles.reshape((angles.shape[0],) + ones_tail + (half_dim,))
    cosine = jnp.cos(angles)
    sine_vals = jnp.sin(angles)
    front_half = values[..., :half_dim]
    back_half = values[..., half_dim:]
    return jnp.concatenate(
        [front_half * cosine - back_half * sine_vals, back_half * cosine + front_half * sine_vals],
        axis=-1,
    )


def norm_rotate(values, gain_vec, position):
    return rotate(values * rms_inv(values) * gain_vec, position)


def pick_rows(wanted, shard_rows):
    targets = jnp.arange(shard_rows.shape[0], dtype=jnp.int32)
    selector = (wanted[:, None] == targets[None, :]).astype(jnp.bfloat16)
    return jnp.dot(selector, shard_rows, preferred_element_type=jnp.float32)


def body(
    hidden,
    deal_order,
    lengths,
    page_table,
    key_cache,
    value_cache,
    attn_gain,
    w_query,
    w_key,
    w_value,
    w_gate,
    w_out,
    query_gain,
    key_gain,
    mlp_gain,
    mlp_gate,
    mlp_up,
    mlp_down,
):
    local_rows, model_width = hidden.shape
    req_devices = lax.axis_size("req")
    req_index = lax.axis_index("req")
    all_rows = local_rows * req_devices
    head_width = query_gain.shape[0]
    pool_pages = key_cache.shape[0]
    page_size = key_cache.shape[1]
    local_kv = key_cache.shape[2]
    group_size = w_query.shape[1] // (local_kv * head_width)
    scale_factor = 1.0 / math.sqrt(head_width)
    first_own = req_index * local_rows
    hidden_f = hidden.astype(jnp.float32)
    normed = (hidden_f * rms_inv(hidden_f) * attn_gain).astype(jnp.bfloat16)
    own_requests = lax.dynamic_slice_in_dim(deal_order, first_own, local_rows)
    position = lengths[own_requests].astype(jnp.float32)
    queries = jnp.dot(normed, w_query, preferred_element_type=jnp.float32).reshape(
        local_rows, local_kv, group_size, head_width
    )
    queries = norm_rotate(queries, query_gain, position).astype(jnp.bfloat16)
    new_keys = jnp.dot(normed, w_key, preferred_element_type=jnp.float32).reshape(
        local_rows, local_kv, head_width
    )
    new_keys = norm_rotate(new_keys, key_gain, position).astype(jnp.bfloat16)
    new_values = (
        jnp.dot(normed, w_value, preferred_element_type=jnp.float32)
        .astype(jnp.bfloat16)
        .reshape(local_rows, local_kv, head_width)
    )
    gate_logits = jnp.dot(normed, w_gate, preferred_element_type=jnp.float32)
    all_queries = lax.all_gather(queries, "req", axis=0, tiled=True)
    dealt_lengths = lengths[deal_order]
    dealt_tables = page_table[deal_order]
    page_counts = (dealt_lengths + page_size - 1) // page_size
    slot_ids = jnp.arange(dealt_tables.shape[1], dtype=jnp.int32)
    local_ids = dealt_tables - req_index * pool_pages
    usable = (
        (slot_ids[None, :] < page_counts[:, None]) & (local_ids >= 0) & (local_ids < pool_pages)
    )
    targets = jnp.where(usable, local_ids, pool_pages).reshape(-1)
    request_ids = jnp.broadcast_to(
        jnp.arange(all_rows, dtype=jnp.int32)[:, None], dealt_tables.shape
    ).reshape(-1)
    slot_flat = jnp.broadcast_to(slot_ids[None, :], dealt_tables.shape).reshape(-1)
    owners = jnp.full((pool_pages,), all_rows, jnp.int32).at[targets].set(request_ids, mode="drop")
    owner_slots = jnp.zeros((pool_pages,), jnp.int32).at[targets].set(slot_flat, mode="drop")
    safe_owners = jnp.minimum(owners, all_rows - 1)
    filled = jnp.where(
        owners < all_rows,
        jnp.clip(dealt_lengths[safe_owners] - owner_slots * page_size, 0, page_size),
        0,
    )
    page_queries = all_queries[safe_owners]
    scores = (
        jnp.einsum("pkgd,ptkd->pkgt", page_queries, key_cache, preferred_element_type=jnp.float32)
        * scale_factor
    )
    live_mask = (
        jnp.arange(page_size, dtype=jnp.int32)[None, None, None, :] < filled[:, None, None, None]
    )
    scores = jnp.where(live_mask, scores, LOW_SCORE)
    page_peaks = jnp.max(scores, axis=-1)
    local_peaks = (
        jnp.full((all_rows, local_kv, group_size), LOW_SCORE, jnp.float32)
        .at[owners]
        .max(page_peaks, mode="drop")
    )
    self_scores = (
        jnp.einsum("rkgd,rkd->rkg", queries, new_keys, preferred_element_type=jnp.float32)
        * scale_factor
    )
    own_peaks = jnp.maximum(
        lax.dynamic_slice_in_dim(local_peaks, first_own, local_rows), self_scores
    )
    with_self = lax.dynamic_update_slice_in_dim(local_peaks, own_peaks, first_own, 0)
    global_peaks = lax.pmax(with_self, "req")
    global_shift = LOG_TWO * jnp.ceil(global_peaks / LOG_TWO)
    weights = jnp.where(live_mask, jnp.exp(scores - global_shift[safe_owners][..., None]), 0.0)
    totals = (
        jnp.zeros((all_rows, local_kv, group_size), jnp.float32)
        .at[owners]
        .add(jnp.sum(weights, axis=-1), mode="drop")
    )
    page_numerators = jnp.einsum(
        "pkgt,ptkd->pkgd",
        weights.astype(jnp.bfloat16),
        value_cache,
        preferred_element_type=jnp.float32,
    )
    numerators = (
        jnp.zeros((all_rows, local_kv, group_size, head_width), jnp.float32)
        .at[owners]
        .add(page_numerators, mode="drop")
    )
    totals, numerators = (totals, numerators)
    own_totals, own_numerators = (
        lax.psum_scatter(totals, "req", scatter_dimension=0, tiled=True),
        lax.psum_scatter(numerators, "req", scatter_dimension=0, tiled=True),
    )
    own_shift = lax.dynamic_slice_in_dim(global_shift, first_own, local_rows)
    self_weight = jnp.exp(self_scores - own_shift)
    own_totals = own_totals + self_weight
    self_rounded = lax.optimization_barrier(self_weight.astype(jnp.bfloat16)).astype(jnp.float32)
    own_numerators = (
        own_numerators + self_rounded[..., None] * new_values.astype(jnp.float32)[:, :, None, :]
    )
    heads_out = (own_numerators / own_totals[..., None]).reshape(
        local_rows, local_kv * group_size * head_width
    )
    attended = (heads_out * jax.nn.sigmoid(gate_logits)).astype(jnp.bfloat16)
    projected = jnp.dot(attended, w_out, preferred_element_type=jnp.float32)
    attn_total = lax.psum(projected.astype(jnp.bfloat16), "head").astype(jnp.float32)
    mixed_rows = (hidden_f + attn_total).astype(jnp.bfloat16)
    mixed_f = mixed_rows.astype(jnp.float32)
    normed_two = (mixed_f * rms_inv(mixed_f) * mlp_gain).astype(jnp.bfloat16)
    gate_part = jnp.dot(normed_two, mlp_gate, preferred_element_type=jnp.float32)
    up_part = jnp.dot(normed_two, mlp_up, preferred_element_type=jnp.float32)
    inner_act = (jax.nn.silu(gate_part) * up_part).astype(jnp.bfloat16)
    down_part = jnp.dot(inner_act, mlp_down, preferred_element_type=jnp.float32)
    inverse_order = (
        jnp.zeros((all_rows,), jnp.int32).at[deal_order].set(jnp.arange(all_rows, dtype=jnp.int32))
    )
    wanted = lax.dynamic_slice_in_dim(inverse_order, first_own, local_rows)
    mlp_total = lax.psum(down_part.astype(jnp.bfloat16), "head").astype(jnp.float32)
    result = (mixed_f + mlp_total).astype(jnp.bfloat16)
    gathered = pick_rows(wanted, lax.all_gather(result, "req", axis=0, tiled=True))
    output = gathered.astype(jnp.bfloat16)
    return output


def solution(mesh):
    return jax.shard_map(
        body,
        mesh=mesh,
        in_specs=(
            P("req", None),
            P(),
            P(),
            P(),
            P("req", None, "head", None),
            P("req", None, "head", None),
            P(),
            P(None, "head"),
            P(None, "head"),
            P(None, "head"),
            P(None, "head"),
            P("head", None),
            P(),
            P(),
            P(),
            P(None, "head"),
            P(None, "head"),
            P("head", None),
        ),
        out_specs=P("req", None),
        check_vma=False,
    )
```

profile of v0, /device:TPU:2, one launch (start us, length us, event | category | flops | bytes accessed | tf_op | source)
XLA Modules:
  0.0 1038.4 jit_solution(14262938876819041306)
XLA Ops:
  6.6 0.8 compare_select_fusion.1
  7.5 0.8 compare_select_fusion.2
  8.3 1.0 fusion.17
  9.3 3.6 gather_fusion
  12.9 0.7 gather_fusion.3
  13.6 0.3 fusion.77
  14.0 0.1 iota_compare_fusion
  14.2 0.1 lt.102
  14.3 0.1 multiply_cosine_fusion.1
  14.7 52.5 %all_gather.6 = bf16[512,1,2,128]{3,2,1,0:T(2,128)(2,1)S(1)} all-gather(bf16[16,1,2,128]{3,2,1,0:T(2,128)(2,1)S(1)} %pad_maximum_fusion), channel_id=1, replica_groups=mesh['req'=32,'head'=8] {'req'}, dimensions={0}, use_global_device_ids=true | all-gather | bytes 270336 | tf_op jit(solution)/shard_map/all_gather | solution.py:93
  67.2 0.1 copy.63
  67.3 1.0 gather_fusion.1
  68.4 0.2 sub.57
  68.9 0.4 compare_select_fusion
  69.3 120.0 %scatter_custom_fusion.2 = s32[64]{0:T(128)S(1)} fusion(s32[32768]{0:T(1024)S(1)} %bitcast.102, s32[32768]{0:T(1024)S(1)} %reshape.511, s32[]{:T(128)} %constant.24.clone.1), kind=kCustom, calls=%fused_computation.126 | custom fusion | bytes 260 | tf_op jit(solution)/shard_map/scatter | solution.py:108
  189.3 120.0 %scatter_custom_fusion.1 = s32[64]{0:T(128)S(1)} fusion(s32[32768]{0:T(1024)S(1)} %bitcast.103, s32[32768]{0:T(1024)S(1)} %reshape.503, s32[]{:T(128)} %constant.25.clone.1), kind=kCustom, calls=%fused_computation.128 | custom fusion | bytes 260 | tf_op jit(solution)/shard_map/scatter | solution.py:107
  309.4 0.8 gather_fusion.2
  310.2 0.6 gather_fusion.4
  310.9 1.3 fusion.80
  312.2 0.9 scatter_custom_fusion.3
  313.2 0.4 multiply_reduce_fusion.1
  313.7 0.1 fusion.56
  313.9 0.2 fusion.53
  314.2 0.1 dynamic_update_slice.3
  314.4 72.4 %pmax.7 = f32[512,1,2]{0,2,1:T(2,128)S(1)} all-reduce(f32[512,1,2]{0,2,1:T(2,128)S(1)} %dynamic_update_slice.3), channel_id=1, replica_groups=mesh['req'=32,'head'=8] {'req'}, use_global_device_ids=true, to_apply=%region_8.9 | all-reduce | flops 1024 | bytes 8192 | tf_op jit(solution)/shard_map/pmax | solution.py:138
  386.7 0.1 copy.68
  386.9 0.6 gather_fusion.5
  387.5 0.2 fusion.70
  387.7 1.5 scatter_custom_fusion.5
  389.3 2.3 fusion
  391.6 0.1 broadcast.362
  391.8 2.8 scatter_fusion
  394.6 0.8 copy.88
  395.5 0.2 fusion.16
  395.7 203.3 %reduce-scatter.10.cloned.1.call-done = f32[16,2]{1,0:T(8,128)} async-done(((f32[512,2]{1,0:T(8,128)}), f32[16,2]{1,0:T(8,128)}) %reduce-scatter.10.cloned.1.call-update) | async-done | bytes 144
  599.0 0.8 copy.77
  600.0 214.6 %reduce-scatter.8.cloned.1.call-done = f32[16,256]{1,0:T(8,128)} async-done(((f32[512,256]{1,0:T(8,128)}), f32[16,256]{1,0:T(8,128)}) %reduce-scatter.8.cloned.1.call-update) | async-done | bytes 16400
  814.7 0.7 reshape.564
  815.5 3.0 convolution_convert_fusion.2
  818.5 60.0 %all-reduce.3.cloned.1.call-done = bf16[16,2048]{1,0:T(8,128)(2,1)} async-done(((bf16[16,2048]{1,0:T(8,128)(2,1)}), bf16[16,2048]{1,0:T(8,128)(2,1)}) %all-reduce.3.cloned.1.call-update) | async-done | bytes 65552 | tf_op jit(solution)/shard_map/psum | solution.py:174
  878.5 1.0 fusion.21
  879.5 1.8 fusion.41
  881.3 3.3 convolution_convert_fusion.1
  884.7 62.9 %all-reduce.5.cloned.1.call-done = bf16[16,2048]{1,0:T(8,128)(2,1)} async-done(((bf16[16,2048]{1,0:T(8,128)(2,1)}), bf16[16,2048]{1,0:T(8,128)(2,1)}) %all-reduce.5.cloned.1.call-update) | async-done | bytes 65552 | tf_op jit(solution)/shard_map/psum | solution.py:186
  947.6 1.5 fusion.24
  949.1 2.4 scatter_custom_fusion
  951.6 77.6 %all-gather.2.cloned.1.call-done = bf16[512,2048]{1,0:T(8,128)(2,1)} async-done(((bf16[16,2048]{1,0:T(8,128)(2,1)}), bf16[512,2048]{1,0:T(8,128)(2,1)}) %all-gather.2.cloned.1.call-update) | async-done | bytes 2097168 | tf_op jit(solution)/shard_map/all_gather | solution.py:188
  1029.2 2.6 convolution_convert_fusion
  (70 shorter events, 2.0 us)
Async XLA Ops:
  6.5 304.4 %copy-start = (bf16[64,128,1,128]{3,1,2,0:T(8,128)(2,1)S(1)}, bf16[64,128,1,128]{3,1,2,0:T(8,128)(2,1)}, u32[]{:S(2)}) copy-start(bf16[64,128,1,128]{3,1,2,0:T(8,128)(2,1)} %param.22) | copy-start | bytes 6291460
  6.5 7.1 copy-start.2
  6.5 6.4 copy-start.1
  6.5 7.1 copy-start.6
  6.5 7.1 copy-start.3
  6.5 592.5 %reduce-scatter.10.cloned.1.call-start = ((), (), s32[]{:S(2)}) async-start(), calls=%async_computation.6 | async-start | bytes 270336
  9.2 5.2 copy-start.10
  12.9 54.3 %copy-start.7 = (s32[512,64]{0,1:T(8,128)S(1)}, s32[512,64]{0,1:T(8,128)}, u32[]{:S(2)}) copy-start(s32[512,64]{0,1:T(8,128)} %param.21) | copy-start | bytes 393220
  309.3 3.9 copy-start.4
  310.9 2.7 copy-start.9
  389.3 425.4 %reduce-scatter.8.cloned.1.call-start = ((), (), s32[]{:S(2)}) async-start(), calls=%async_computation.5 | async-start | bytes 540672
  391.6 3.9 copy-start.5
  395.4 484.1 %copy-start.8 = (f32[2048]{0:T(1024)S(1)}, f32[2048]{0:T(1024)}, u32[]{:S(2)}) copy-start(f32[2048]{0:T(1024)} %param.32) | copy-start | bytes 24580
  395.4 483.1 %all-reduce.3.cloned.1.call-start = ((), (), s32[]{:S(2)}) async-start(), calls=%async_computation.2 | async-start | bytes 131072 | tf_op jit(solution)/shard_map/psum | solution.py:174
  818.5 129.1 %all-reduce.5.cloned.1.call-start = ((), (), s32[]{:S(2)}) async-start(), calls=%async_computation.3 | async-start | bytes 131072 | tf_op jit(solution)/shard_map/psum | solution.py:186
  884.6 144.6 %all-gather.2.cloned.1.call-start = ((), (), s32[]{:S(2)}) async-start(), calls=%async_computation.4 | async-start | bytes 2162688 | tf_op jit(solution)/shard_map/all_gather | solution.py:188
Sparse Core Ops, SparseCore 0:
  389.4 209.5 reduce-scatter.9
  603.3 211.3 reduce-scatter.7
  818.6 59.8 all-reduce.2
  884.7 62.8 all-reduce.4
  950.0 79.1 all-gather.1
where the time goes:
time: 1040 us
  waiting for transfers between devices  619 us (60%)
  local copies, waits for them, and re-layouts  254 us (24%)
  blocking collectives  125 us (12%)
  matrix products  15.3 us (1%)
  between operations  13.5 us (1%)
  other arithmetic  12.2 us (1%)
    unnamed x7, waiting for transfers between devices  418 us
    scatter x1, local copies, waits for them, and re-layouts, body(): jnp.zeros((pool_pages,), jnp.int32).at[targets].set(slot_flat, mode='drop')  120 us
    scatter x1, local copies, waits for them, and re-layouts, body(): jnp.full((pool_pages,), all_rows, jnp.int32).at[targets]  120 us
    all_gather x1, waiting for transfers between devices, body(): lax.all_gather(result, 'req', axis=0, tiled=True)  77.6 us
    pmax x1, blocking collectives, body(): global_peaks = lax.pmax(with_self, 'req')  72.4 us
    psum x1, waiting for transfers between devices, body(): lax.psum(down_part.astype(jnp.bfloat16), 'head').astype(jnp.float32)  62.9 us
    psum x1, waiting for transfers between devices, body(): lax.psum(projected.astype(jnp.bfloat16), 'head').astype(jnp.float32)  60 us
    all_gather x1, blocking collectives, body(): all_queries = lax.all_gather(queries, 'req', axis=0, tiled=True)  52.5 us
  transfers between devices with their start and end apart: 5, of which 5 were waited for; matrix products, arithmetic and copies ran while one was open for 1% of the time, Pallas kernels for 0%

commit v1 on v0

--- a/solution.py
+++ b/solution.py
@@ -1,3 +1,4 @@
+import functools
 import math
 import jax
 import jax.numpy as jnp
@@ -8,6 +9,14 @@
 ROPE_BASE = 1000000.0
 LOW_SCORE = -1e30
 LOG_TWO = math.log(2.0)
+
+
+def _close_local_data(t0, across):
+    view_out = jax.lax.all_gather(t0, across)
+    return jnp.sum(view_out, axis=0)
+
+
+hold_plate = functools.partial(_close_local_data, across="head")
 
 
 def rms_inv(values):
@@ -183,7 +192,7 @@
         jnp.zeros((all_rows,), jnp.int32).at[deal_order].set(jnp.arange(all_rows, dtype=jnp.int32))
     )
     wanted = lax.dynamic_slice_in_dim(inverse_order, first_own, local_rows)
-    mlp_total = lax.psum(down_part.astype(jnp.bfloat16), "head").astype(jnp.float32)
+    mlp_total = hold_plate(down_part.astype(jnp.bfloat16)).astype(jnp.float32)
     result = (mixed_f + mlp_total).astype(jnp.bfloat16)
     gathered = pick_rows(wanted, lax.all_gather(result, "req", axis=0, tiled=True))
     output = gathered.astype(jnp.bfloat16)

time: 1040 us -> 988 us (0.950)
  waiting for transfers between devices: 619 us -> 556 us
  blocking collectives: 125 us -> 138 us
    psum x1 -> x0, waiting for transfers between devices: 62.9 us -> none  [body(): lax.psum(down_part.astype(jnp.bfloat16), 'head').astype(jnp.float32)]
    all_gather x0 -> x1, blocking collectives: none -> 13.1 us  [_close_local_data(): view_out = jax.lax.all_gather(t0, across)]
    unnamed x7 -> x6, waiting for transfers between devices: 418 us -> 418 us
  transfers between devices with their start and end apart: 5 -> 4, of which waited for: 5 -> 4; matrix products, arithmetic and copies ran while one was open for 1% -> 1% of each run, Pallas kernels for 0% -> 0%
where the time goes in v1:
time: 988 us; the launch traced here: 987 us
  waiting for transfers between devices  556 us (56%)
  local copies, waits for them, and re-layouts  254 us (26%)
  blocking collectives  138 us (14%)
  matrix products  14.7 us (1%)
  between operations  13.5 us (1%)
  other arithmetic  11.4 us (1%)
    unnamed x6, waiting for transfers between devices  418 us
    scatter x1, local copies, waits for them, and re-layouts, body(): jnp.zeros((pool_pages,), jnp.int32).at[targets].set(slot_flat, mode='drop')  120 us
    scatter x1, local copies, waits for them, and re-layouts, body(): jnp.full((pool_pages,), all_rows, jnp.int32).at[targets]  120 us
    all_gather x1, waiting for transfers between devices, body(): lax.all_gather(result, 'req', axis=0, tiled=True)  77.6 us
    pmax x1, blocking collectives, body(): global_peaks = lax.pmax(with_self, 'req')  72.4 us
    psum x1, waiting for transfers between devices, body(): lax.psum(projected.astype(jnp.bfloat16), 'head').astype(jnp.float32)  60 us
    all_gather x1, blocking collectives, body(): all_queries = lax.all_gather(queries, 'req', axis=0, tiled=True)  52.5 us
  transfers between devices with their start and end apart: 4, of which 4 were waited for; matrix products, arithmetic and copies ran while one was open for 1% of the time, Pallas kernels for 0%

profile of v1, /device:TPU:2, one launch (start us, length us, event | category | flops | bytes accessed | tf_op | source)
XLA Modules:
  0.0 987.1 jit_solution(17392821684033142270)
XLA Ops:
  6.6 0.8 compare_select_fusion.1
  7.5 0.8 compare_select_fusion.2
  8.3 1.0 fusion.17
  9.3 3.6 gather_fusion
  12.9 0.7 gather_fusion.3
  13.6 0.3 fusion.77
  14.0 0.1 iota_compare_fusion
  14.2 0.1 lt.102
  14.3 0.1 multiply_cosine_fusion.1
  14.7 52.5 %all_gather.12 = bf16[512,1,2,128]{3,2,1,0:T(2,128)(2,1)S(1)} all-gather(bf16[16,1,2,128]{3,2,1,0:T(2,128)(2,1)S(1)} %pad_maximum_fusion), channel_id=1, replica_groups=mesh['req'=32,'head'=8] {'req'}, dimensions={0}, use_global_device_ids=true | all-gather | bytes 270336 | tf_op jit(solution)/shard_map/all_gather | solution.py:102
  67.2 0.1 copy.63
  67.3 1.0 gather_fusion.1
  68.4 0.2 sub.57
  68.9 0.4 compare_select_fusion
  69.3 120.0 %scatter_custom_fusion.2 = s32[64]{0:T(128)S(1)} fusion(s32[32768]{0:T(1024)S(1)} %bitcast.104, s32[32768]{0:T(1024)S(1)} %reshape.511, s32[]{:T(128)} %constant.25.clone.1), kind=kCustom, calls=%fused_computation.126 | custom fusion | bytes 260 | tf_op jit(solution)/shard_map/scatter | solution.py:117
  189.3 120.0 %scatter_custom_fusion.1 = s32[64]{0:T(128)S(1)} fusion(s32[32768]{0:T(1024)S(1)} %bitcast.105, s32[32768]{0:T(1024)S(1)} %reshape.503, s32[]{:T(128)} %constant.26.clone.1), kind=kCustom, calls=%fused_computation.128 | custom fusion | bytes 260 | tf_op jit(solution)/shard_map/scatter | solution.py:116
  309.4 0.8 gather_fusion.2
  310.2 0.6 gather_fusion.4
  310.9 1.3 fusion.80
  312.2 0.9 scatter_custom_fusion.3
  313.2 0.4 multiply_reduce_fusion.1
  313.7 0.1 fusion.56
  313.9 0.2 fusion.53
  314.2 0.1 dynamic_update_slice.3
  314.4 72.4 %pmax.7 = f32[512,1,2]{0,2,1:T(2,128)S(1)} all-reduce(f32[512,1,2]{0,2,1:T(2,128)S(1)} %dynamic_update_slice.3), channel_id=1, replica_groups=mesh['req'=32,'head'=8] {'req'}, use_global_device_ids=true, to_apply=%region_8.9 | all-reduce | flops 1024 | bytes 8192 | tf_op jit(solution)/shard_map/pmax | solution.py:147
  386.7 0.1 copy.68
  386.9 0.6 gather_fusion.5
  387.5 0.2 fusion.70
  387.7 1.5 scatter_custom_fusion.5
  389.3 2.3 fusion
  391.6 0.1 broadcast.362
  391.8 2.8 scatter_fusion
  394.6 0.8 copy.88
  395.5 0.2 fusion.16
  395.7 203.3 %reduce-scatter.10.cloned.1.call-done = f32[16,2]{1,0:T(8,128)} async-done(((f32[512,2]{1,0:T(8,128)}), f32[16,2]{1,0:T(8,128)}) %reduce-scatter.10.cloned.1.call-update) | async-done | bytes 144
  599.0 0.8 copy.77
  600.0 214.6 %reduce-scatter.8.cloned.1.call-done = f32[16,256]{1,0:T(8,128)} async-done(((f32[512,256]{1,0:T(8,128)}), f32[16,256]{1,0:T(8,128)}) %reduce-scatter.8.cloned.1.call-update) | async-done | bytes 16400
  814.7 0.7 reshape.565
  815.5 3.0 convolution_convert_fusion.2
  818.5 60.0 %all-reduce.2.cloned.1.call-done = bf16[16,2048]{1,0:T(8,128)(2,1)} async-done(((bf16[16,2048]{1,0:T(8,128)(2,1)}), bf16[16,2048]{1,0:T(8,128)(2,1)}) %all-reduce.2.cloned.1.call-update) | async-done | bytes 65552 | tf_op jit(solution)/shard_map/psum | solution.py:183
  878.5 1.0 fusion.21
  879.5 1.8 fusion.41
  881.3 2.7 convolution_convert_fusion.1
  883.9 13.1 %all-gather = bf16[128,2048]{1,0:T(8,128)(2,1)S(1)} all-gather(bf16[16,2048]{1,0:T(8,128)(2,1)S(1)} %convolution_convert_fusion.1), channel_id=2, replica_groups=mesh['req'=32,'head'=8] {'head'}, dimensions={0}, use_global_device_ids=true | all-gather | bytes 589824 | tf_op jit(solution)/shard_map/all_gather | solution.py:15
  897.1 0.6 fusion.24
  897.8 2.4 scatter_custom_fusion
  900.3 77.6 %all-gather.3.cloned.1.call-done = bf16[512,2048]{1,0:T(8,128)(2,1)} async-done(((bf16[16,2048]{1,0:T(8,128)(2,1)}), bf16[512,2048]{1,0:T(8,128)(2,1)}) %all-gather.3.cloned.1.call-update) | async-done | bytes 2097168 | tf_op jit(solution)/shard_map/all_gather | solution.py:197
  977.9 2.6 convolution_convert_fusion
  (69 shorter events, 2.0 us)
Async XLA Ops:
  6.5 304.4 %copy-start = (bf16[64,128,1,128]{3,1,2,0:T(8,128)(2,1)S(1)}, bf16[64,128,1,128]{3,1,2,0:T(8,128)(2,1)}, u32[]{:S(2)}) copy-start(bf16[64,128,1,128]{3,1,2,0:T(8,128)(2,1)} %param.22) | copy-start | bytes 6291460
  6.5 7.1 copy-start.2
  6.5 6.4 copy-start.1
  6.5 7.1 copy-start.6
  6.5 7.1 copy-start.3
  6.5 592.5 %reduce-scatter.10.cloned.1.call-start = ((), (), s32[]{:S(2)}) async-start(), calls=%async_computation.5 | async-start | bytes 270336
  9.2 5.2 copy-start.10
  12.9 54.3 %copy-start.7 = (s32[512,64]{0,1:T(8,128)S(1)}, s32[512,64]{0,1:T(8,128)}, u32[]{:S(2)}) copy-start(s32[512,64]{0,1:T(8,128)} %param.21) | copy-start | bytes 393220
  309.3 3.9 copy-start.4
  310.9 2.7 copy-start.9
  389.3 425.4 %reduce-scatter.8.cloned.1.call-start = ((), (), s32[]{:S(2)}) async-start(), calls=%async_computation.4 | async-start | bytes 540672
  391.6 3.9 copy-start.5
  395.4 484.1 %copy-start.8 = (f32[2048]{0:T(1024)S(1)}, f32[2048]{0:T(1024)}, u32[]{:S(2)}) copy-start(f32[2048]{0:T(1024)} %param.32) | copy-start | bytes 24580
  395.4 483.1 %all-reduce.2.cloned.1.call-start = ((), (), s32[]{:S(2)}) async-start(), calls=%async_computation.2 | async-start | bytes 131072 | tf_op jit(solution)/shard_map/psum | solution.py:183
  818.5 159.4 %all-gather.3.cloned.1.call-start = ((), (), s32[]{:S(2)}) async-start(), calls=%async_computation.3 | async-start | bytes 2162688 | tf_op jit(solution)/shard_map/all_gather | solution.py:197
Sparse Core Ops, SparseCore 0:
  389.4 209.5 reduce-scatter.9
  603.3 211.3 reduce-scatter.7
  818.6 59.8 all-reduce.1
  897.9 79.9 all-gather.2
